TPU v7x, 512 devices: a whole 4x8x8 slice. The times are simulated.
512 devices in a mesh: mem: 32 (over x, y_lo, core), tile: 16 (over z, y_hi).
Axes of the slice: x: 4, y: 8 (y_hi: 2, y_lo: 4; y = y_hi * 4 + y_lo), z: 8, core: 2. Of those that a mesh axis runs over, the one named last changes fastest.
Arguments:
- background: float32 [256, 2048, 256], P('mem', 'tile'), may hold values from -6 to 6
- diffusion: float32 [256], replicated, may hold values from 0.05 to 0.2
- advection: float32 [256], replicated, may hold values from -0.25 to 0.25
- obs_where: int32 [16, 128, 512], P('tile'), may hold values from 0 to 255
- obs_count: int32 [16, 128], P('tile'), may hold values from 256 to 512
- obs_value: float32 [16, 128, 512], P('tile'), may hold values from -6 to 6
- obs_rinv: float32 [16, 128, 512], P('tile'), may hold values from 1 to 1000
Outputs:
- analysis: float32 [256, 2048, 256], P('mem', 'tile')
Inputs may be any that keep to these rules, and one draw needn't show every extreme that they name: `obs_where`: each slot reads one entry of its column's 4 * 64 state entries. A column uses its first obs_count slots.
All inputs are finite; a program needn't handle non-finite values.
Results may differ from a plain program's by a relative error of at most 0.0003.
Values sent between devices are 32-bit elements; how exact they have to be, the bound alone decides.
A program may use at most 64 MiB of HBM per device.

v0:
```python
import jax
import jax.numpy as jnp
from jax import lax
from jax.sharding import PartitionSpec as P

ITERS = 12


HIGH = lax.Precision.HIGHEST


def extended(cells, sides, width):
    for axis, dim in sides:
        count = lax.axis_size(axis)
        head = lax.slice_in_dim(cells, 0, width, axis=dim)
        tail = lax.slice_in_dim(cells, cells.shape[dim] - width, cells.shape[dim], axis=dim)
        cells = jnp.concatenate(
            [
                lax.ppermute(tail, axis, [(i, (i + 1) % count) for i in range(count)]),
                cells,
                lax.ppermute(head, axis, [((i + 1) % count, i) for i in range(count)]),
            ],
            axis=dim,
        )
    return cells


def analyse(states, where, count, value, rinv):
    members = states.shape[0]
    entries = states.shape[2]
    slots = where.shape[1]
    mean = jnp.mean(states, axis=0)
    anomaly = states - mean[None]
    mask = (jnp.arange(slots, dtype=jnp.int32)[None, :] < count[:, None]).astype(jnp.float32)
    onehot = (where[:, :, None] == jnp.arange(entries, dtype=jnp.int32)[None, None, :]).astype(
        jnp.float32
    ) * mask[:, :, None]
    yb = jnp.einsum("npv,knv->npk", onehot, anomaly, precision=HIGH)
    innov = value - jnp.einsum("npv,nv->np", onehot, mean, precision=HIGH)
    weight_obs = rinv * mask
    eye = jnp.eye(members, dtype=jnp.float32)
    gram = (members - 1.0) * eye[None] + jnp.einsum(
        "npk,npl->nkl", yb * weight_obs[:, :, None], yb, precision=HIGH
    )
    scale = jnp.sqrt(jnp.sum(gram * gram, axis=(1, 2)))
    start_y = gram / scale[:, None, None]
    start_z = jnp.broadcast_to(eye[None], gram.shape)

    def newton(step, carry):
        iter_y, iter_z = carry
        middle = 1.5 * eye[None] - 0.5 * jnp.einsum("nij,njk->nik", iter_z, iter_y, precision=HIGH)
        return (
            jnp.einsum("nij,njk->nik", iter_y, middle, precision=HIGH),
            jnp.einsum("nij,njk->nik", middle, iter_z, precision=HIGH),
        )

    final_y, final_z = lax.fori_loop(0, ITERS, newton, (start_y, start_z))
    weights = jnp.sqrt(members - 1.0) * final_z / jnp.sqrt(scale)[:, None, None]
    project = jnp.einsum("npk,np->nk", yb, weight_obs * innov, precision=HIGH)
    inner = jnp.einsum("nkl,nl->nk", final_z, project, precision=HIGH)
    wmean = jnp.einsum("nkl,nl->nk", final_z, inner, precision=HIGH) / scale[:, None]
    trans = weights + wmean[:, :, None]
    return mean[None] + jnp.einsum("nij,inv->jnv", trans, anomaly, precision=HIGH)


def advance_padded(padded, diffusion, advection):
    middle = padded[:, 1:-1]
    left = padded[:, :-2]
    right = padded[:, 2:]
    return middle + diffusion * (left - 2.0 * middle + right) + advection * (0.5 * (left - right))


def body(background, diffusion, advection, obs_where, obs_count, obs_value, obs_rinv):
    state = background
    padded = extended(state, (("tile", 1),), 2)
    padded = advance_padded(padded, diffusion, advection)
    state = advance_padded(padded, diffusion, advection)
    local_members = state.shape[0]
    tile_cols = state.shape[1]
    entries = state.shape[2]
    groups = lax.axis_size("mem")
    per_owner = tile_cols // groups
    blocks = state.reshape(local_members, groups, per_owner, entries)
    owned = lax.all_to_all(blocks, "mem", split_axis=1, concat_axis=0, tiled=True)
    offset = lax.axis_index("mem") * per_owner
    where = lax.dynamic_slice_in_dim(obs_where[0], offset, per_owner, 0)
    count = lax.dynamic_slice_in_dim(obs_count[0], offset, per_owner, 0)
    value = lax.dynamic_slice_in_dim(obs_value[0], offset, per_owner, 0)
    rinv = lax.dynamic_slice_in_dim(obs_rinv[0], offset, per_owner, 0)
    result = analyse(owned[:, 0], where, count, value, rinv)
    back = lax.all_to_all(result[:, None], "mem", split_axis=0, concat_axis=1, tiled=True)
    return back.reshape(local_members, tile_cols, entries)


def solution(mesh):
    return jax.shard_map(
        body,
        mesh=mesh,
        in_specs=(
            P("mem", "tile", None),
            P(),
            P(),
            P("tile", None, None),
            P("tile", None),
            P("tile", None, None),
            P("tile", None, None),
        ),
        out_specs=P("mem", "tile", None),
        check_vma=False,
    )
```

profile of v0, /device:TPU:1, one launch (start us, length us, event | category | flops | bytes accessed | tf_op | source)
XLA Modules:
  0.0 161.4 jit_solution(13977318619464913238)
XLA Ops:
  0.0 1.9 %copy.41 = f32[8,128,256]{2,0,1:T(8,128)S(1)} copy(f32[8,128,256]{2,1,0:T(8,128)} %param.9) | data formatting | bytes 2097152 | tf_op args[0]
  2.0 8.3 %collective-permute-start = (f32[8,2,256]{2,0,1:T(8,128)S(1)}, f32[8,2,256]{2,0,1:T(8,128)S(1)}, u32[]{:S(2)}, u32[]{:S(2)}) collective-permute-start(f32[8,2,256]{2,0,1:T(8,128)S(1)} %get-tuple-element.57), channel_id=1, source_target_pairs={{0,1},{1,2},{2,3},{3,4},{4,5},{5,6},{6,7},{7,8},{8,9},{9,10},{10,1... | collective-permute-start | bytes 49160 | tf_op jit(solution)/shard_map/ppermute | solution.py:19
  10.3 10.4 %collective-permute-start.1 = (f32[8,2,256]{2,0,1:T(8,128)S(1)}, f32[8,2,256]{2,0,1:T(8,128)S(1)}, u32[]{:S(2)}, u32[]{:S(2)}) collective-permute-start(f32[8,2,256]{2,0,1:T(8,128)S(1)} %get-tuple-element.56), channel_id=1, source_target_pairs={{1,0},{2,1},{3,2},{4,3},{5,4},{6,5},{7,6},{8,7},{9,8},{10,9},{11,1... | collective-permute-start | bytes 49160 | tf_op jit(solution)/shard_map/ppermute | solution.py:21
  21.8 1.2 multiply_add_fusion.1
  23.0 6.5 %all-to-all-start = ((f32[8,32,4,256]{3,0,2,1:T(8,128)}), f32[8,32,4,256]{3,0,2,1:T(8,128)S(1)}, u32[]{:S(2)}, u32[]{:S(2)}) async-start(f32[8,32,4,256]{3,0,2,1:T(8,128)} %bitcast), calls=%async_computation | async-start | bytes 2097152 | tf_op jit(solution)/shard_map/all_to_all | solution.py:84
  30.4 26.9 %all-to-all-done = f32[8,32,4,256]{3,0,2,1:T(8,128)S(1)} async-done(((f32[8,32,4,256]{3,0,2,1:T(8,128)}), f32[8,32,4,256]{3,0,2,1:T(8,128)S(1)}, u32[]{:S(2)}, u32[]{:S(2)}) %all-to-all-start) | async-done | bytes 1048608 | tf_op jit(solution)/shard_map/all_to_all | solution.py:84
  57.4 2.3 %fusion.6 = f32[4,1,512]{2,1,0:T(1,128)S(1)} fusion(f32[4,512]{1,0:T(4,128)S(1)} %fusion.35, s32[4,512]{1,0:T(4,128)S(1)} %dynamic-slice_bitcast_fusion, f32[4,256,1]{1,0,2:T(4,128)S(1)} %get-tuple-element.60), kind=kOutput, calls=%fused_computation.8 | convolution fusion | flops 7340032 | bytes 28672 | tf_op jit(solution)/shard_map/npv,nv->np/dot_general | solution.py:39
  60.6 2.5 %fusion.8 = f32[4,512,256]{2,1,0:T(8,128)S(1)} fusion(f32[4,512]{1,0:T(4,128)S(1)} %fusion.35, s32[4,512]{1,0:T(4,128)S(1)} %dynamic-slice_bitcast_fusion, f32[4,256]{1,0:T(4,128)S(1)} %get-tuple-element.61, f32[8,32,4,256]{3,0,2,1:T(8,128)S(1)} %all-to-all-done), kind=kOutput, calls=%fused_computation.10 | convolution fusion | flops 1611923456 | bytes 3166208 | tf_op jit(solution)/shard_map/npv,knv->npk/dot_general | solution.py:38
  63.1 1.2 fusion.33
  64.3 4.0 %multiply_reduce_fusion = (f32[4]{0:T(128)S(1)}, f32[4,256,256]{2,1,0:T(8,128)S(1)}) fusion(f32[4,512,256]{2,1,0:T(8,128)S(1)} %fusion.8, f32[4,512]{1,0:T(4,128)S(1)} %get-tuple-element.55, f32[256,256]{1,0:T(8,128)S(1)} %fusion.30), kind=kOutput, calls=%fused_computation.24 | convolution fusion | flops 1611923456 | bytes 3416080 | tf_op jit(solution)/shard_map/npk,npl->nkl/dot_general | solution.py:42
  69.9 53.8 %while.13 = (s32[]{:T(128)}, f32[4,256,256]{1,2,0:T(8,128)S(1)}, f32[4,256,256]{2,1,0:T(8,128)S(1)}, s32[]{:T(128)}) while((s32[]{:T(128)}, f32[4,256,256]{1,2,0:T(8,128)S(1)}, f32[4,256,256]{2,1,0:T(8,128)S(1)}, s32[]{:T(128)}) %tuple.31), condition=%wide.region_3.0_spmd.clone, body=%wide.region_2.0_spmd.clone.sunk | while | flops 2416574464 | bytes 14155829 | solution.py:57
  70.1 1.2 fusion.76
  71.3 1.1 fusion.77
  72.4 1.9 %convolution_bitcast_fusion.2 = f32[4,256,256]{1,2,0:T(8,128)S(1)} fusion(f32[4,256,256]{2,1,0:T(8,128)S(1)} %fusion.76, f32[4,256,256]{1,2,0:T(8,128)S(1)} %copy.103), kind=kOutput, calls=%fused_computation.1.clone.1 | convolution fusion | flops 805306368 | bytes 3145728 | tf_op jit(solution)/shard_map/while/body/eval_jaxpr/nij,njk->nik/dot_general | solution.py:53
  74.5 1.2 fusion.76
  75.7 1.1 fusion.77
  76.9 1.9 %convolution_bitcast_fusion.2 = f32[4,256,256]{1,2,0:T(8,128)S(1)} fusion(f32[4,256,256]{2,1,0:T(8,128)S(1)} %fusion.76, f32[4,256,256]{1,2,0:T(8,128)S(1)} %copy.103), kind=kOutput, calls=%fused_computation.1.clone.1 | convolution fusion | flops 805306368 | bytes 3145728 | tf_op jit(solution)/shard_map/while/body/eval_jaxpr/nij,njk->nik/dot_general | solution.py:53
  79.0 1.2 fusion.76
  80.2 1.1 fusion.77
  81.4 1.9 %convolution_bitcast_fusion.2 = f32[4,256,256]{1,2,0:T(8,128)S(1)} fusion(f32[4,256,256]{2,1,0:T(8,128)S(1)} %fusion.76, f32[4,256,256]{1,2,0:T(8,128)S(1)} %copy.103), kind=kOutput, calls=%fused_computation.1.clone.1 | convolution fusion | flops 805306368 | bytes 3145728 | tf_op jit(solution)/shard_map/while/body/eval_jaxpr/nij,njk->nik/dot_general | solution.py:53
  83.5 1.2 fusion.76
  84.7 1.1 fusion.77
  85.8 1.9 %convolution_bitcast_fusion.2 = f32[4,256,256]{1,2,0:T(8,128)S(1)} fusion(f32[4,256,256]{2,1,0:T(8,128)S(1)} %fusion.76, f32[4,256,256]{1,2,0:T(8,128)S(1)} %copy.103), kind=kOutput, calls=%fused_computation.1.clone.1 | convolution fusion | flops 805306368 | bytes 3145728 | tf_op jit(solution)/shard_map/while/body/eval_jaxpr/nij,njk->nik/dot_general | solution.py:53
  87.9 1.2 fusion.76
  90.3 1.9 %convolution_bitcast_fusion.2 = f32[4,256,256]{1,2,0:T(8,128)S(1)} fusion(f32[4,256,256]{2,1,0:T(8,128)S(1)} %fusion.76, f32[4,256,256]{1,2,0:T(8,128)S(1)} %copy.103), kind=kOutput, calls=%fused_computation.1.clone.1 | convolution fusion | flops 805306368 | bytes 3145728 | tf_op jit(solution)/shard_map/while/body/eval_jaxpr/nij,njk->nik/dot_general | solution.py:53
  92.4 1.2 fusion.76
  93.6 1.1 fusion.77
  94.8 1.9 %convolution_bitcast_fusion.2 = f32[4,256,256]{1,2,0:T(8,128)S(1)} fusion(f32[4,256,256]{2,1,0:T(8,128)S(1)} %fusion.76, f32[4,256,256]{1,2,0:T(8,128)S(1)} %copy.103), kind=kOutput, calls=%fused_computation.1.clone.1 | convolution fusion | flops 805306368 | bytes 3145728 | tf_op jit(solution)/shard_map/while/body/eval_jaxpr/nij,njk->nik/dot_general | solution.py:53
  96.9 1.2 fusion.76
  98.1 1.1 fusion.77
  99.2 1.9 %convolution_bitcast_fusion.2 = f32[4,256,256]{1,2,0:T(8,128)S(1)} fusion(f32[4,256,256]{2,1,0:T(8,128)S(1)} %fusion.76, f32[4,256,256]{1,2,0:T(8,128)S(1)} %copy.103), kind=kOutput, calls=%fused_computation.1.clone.1 | convolution fusion | flops 805306368 | bytes 3145728 | tf_op jit(solution)/shard_map/while/body/eval_jaxpr/nij,njk->nik/dot_general | solution.py:53
  101.3 1.2 fusion.76
  103.7 1.9 %convolution_bitcast_fusion.2 = f32[4,256,256]{1,2,0:T(8,128)S(1)} fusion(f32[4,256,256]{2,1,0:T(8,128)S(1)} %fusion.76, f32[4,256,256]{1,2,0:T(8,128)S(1)} %copy.103), kind=kOutput, calls=%fused_computation.1.clone.1 | convolution fusion | flops 805306368 | bytes 3145728 | tf_op jit(solution)/shard_map/while/body/eval_jaxpr/nij,njk->nik/dot_general | solution.py:53
  105.8 1.2 fusion.76
  107.0 1.1 fusion.77
  108.2 1.9 %convolution_bitcast_fusion.2 = f32[4,256,256]{1,2,0:T(8,128)S(1)} fusion(f32[4,256,256]{2,1,0:T(8,128)S(1)} %fusion.76, f32[4,256,256]{1,2,0:T(8,128)S(1)} %copy.103), kind=kOutput, calls=%fused_computation.1.clone.1 | convolution fusion | flops 805306368 | bytes 3145728 | tf_op jit(solution)/shard_map/while/body/eval_jaxpr/nij,njk->nik/dot_general | solution.py:53
  110.3 1.2 fusion.76
  111.5 1.1 fusion.77
  112.6 1.9 %convolution_bitcast_fusion.2 = f32[4,256,256]{1,2,0:T(8,128)S(1)} fusion(f32[4,256,256]{2,1,0:T(8,128)S(1)} %fusion.76, f32[4,256,256]{1,2,0:T(8,128)S(1)} %copy.103), kind=kOutput, calls=%fused_computation.1.clone.1 | convolution fusion | flops 805306368 | bytes 3145728 | tf_op jit(solution)/shard_map/while/body/eval_jaxpr/nij,njk->nik/dot_general | solution.py:53
  114.7 1.2 fusion.76
  115.9 1.1 fusion.77
  117.1 1.9 %convolution_bitcast_fusion.2 = f32[4,256,256]{1,2,0:T(8,128)S(1)} fusion(f32[4,256,256]{2,1,0:T(8,128)S(1)} %fusion.76, f32[4,256,256]{1,2,0:T(8,128)S(1)} %copy.103), kind=kOutput, calls=%fused_computation.1.clone.1 | convolution fusion | flops 805306368 | bytes 3145728 | tf_op jit(solution)/shard_map/while/body/eval_jaxpr/nij,njk->nik/dot_general | solution.py:53
  119.2 1.2 fusion.76
  120.4 1.1 fusion.77
  121.6 1.9 %convolution_bitcast_fusion.2 = f32[4,256,256]{1,2,0:T(8,128)S(1)} fusion(f32[4,256,256]{2,1,0:T(8,128)S(1)} %fusion.76, f32[4,256,256]{1,2,0:T(8,128)S(1)} %copy.103), kind=kOutput, calls=%fused_computation.1.clone.1 | convolution fusion | flops 805306368 | bytes 3145728 | tf_op jit(solution)/shard_map/while/body/eval_jaxpr/nij,njk->nik/dot_general | solution.py:53
  125.8 2.1 %fusion.13 = f32[256,1,4,256]{0,3,2,1:T(8,128)S(1)} fusion(f32[4,256,256]{2,1,0:T(8,128)S(1)} %get-tuple-element.27, f32[4,256]{1,0:T(4,128)S(1)} %bitcast_divide_fusion, f32[4]{0:T(128)S(1)} %get-tuple-element.62, f32[4,256]{1,0:T(4,128)S(1)} %get-tuple-element.61, f32[8,32,4,256]{3,0,2,1:T(8,128)S(1)} %all-to-all-done), kind=kOutput, calls=%fused_computation.15 | convolution fusion | flops 806617088 | bytes 3153936 | tf_op jit(solution)/shard_map/nij,inv->jnv/dot_general | solution.py:63
  128.3 31.5 %all_to_all.30 = f32[256,1,4,256]{3,2,1,0:T(4,128)S(1)} all-to-all(f32[256,1,4,256]{3,2,1,0:T(4,128)S(1)} %copy.50), channel_id=1, replica_groups=mesh['mem'=32,'tile'=16] {'mem'}, dimensions={0} | all-to-all | bytes 2097152 | tf_op jit(solution)/shard_map/all_to_all | solution.py:91
  160.1 1.3 copy.53
  (76 shorter events, 11.5 us)
Async XLA Ops:
  0.0 29.6 %copy-start = (s32[1,128,512]{2,1,0:T(8,128)S(1)}, s32[1,128,512]{2,1,0:T(8,128)}, u32[]{:S(2)}) copy-start(s32[1,128,512]{2,1,0:T(8,128)} %param.12) | copy-start | bytes 786436
  0.0 20.7 %copy-start.1 = (f32[8,128,256]{2,1,0:T(8,128)S(1)}, f32[8,128,256]{2,1,0:T(8,128)}, u32[]{:S(2)}) copy-start(f32[8,128,256]{2,1,0:T(8,128)} %param.9) | copy-start | bytes 3145732
  0.0 20.7 %copy-start.3 = (f32[256]{0:T(256)S(1)}, f32[256]{0:T(256)}, u32[]{:S(2)}) copy-start(f32[256]{0:T(256)} %param.11) | copy-start | bytes 3076
  2.0 18.7 %collective-permute-start = (f32[8,2,256]{2,0,1:T(8,128)S(1)}, f32[8,2,256]{2,0,1:T(8,128)S(1)}, u32[]{:S(2)}, u32[]{:S(2)}) collective-permute-start(f32[8,2,256]{2,0,1:T(8,128)S(1)} %get-tuple-element.57), channel_id=1, source_target_pairs={{0,1},{1,2},{2,3},{3,4},{4,5},{5,6},{6,7},{7,8},{8,9},{9,10},{10,1... | collective-permute-start | bytes 49160 | tf_op jit(solution)/shard_map/ppermute | solution.py:19
  10.3 11.3 %collective-permute-start.1 = (f32[8,2,256]{2,0,1:T(8,128)S(1)}, f32[8,2,256]{2,0,1:T(8,128)S(1)}, u32[]{:S(2)}, u32[]{:S(2)}) collective-permute-start(f32[8,2,256]{2,0,1:T(8,128)S(1)} %get-tuple-element.56), channel_id=1, source_target_pairs={{1,0},{2,1},{3,2},{4,3},{5,4},{6,5},{7,6},{8,7},{9,8},{10,9},{11,1... | collective-permute-start | bytes 49160 | tf_op jit(solution)/shard_map/ppermute | solution.py:21
  20.7 0.8 copy-start.2
  23.0 6.5 %copy-start.4 = (s32[1,128]{1,0:T(1,128)S(1)}, s32[1,128]{1,0:T(1,128)}, u32[]{:S(2)}) copy-start(s32[1,128]{1,0:T(1,128)} %param.13) | copy-start | bytes 1540
  23.0 34.3 %all-to-all-start = ((f32[8,32,4,256]{3,0,2,1:T(8,128)}), f32[8,32,4,256]{3,0,2,1:T(8,128)S(1)}, u32[]{:S(2)}, u32[]{:S(2)}) async-start(f32[8,32,4,256]{3,0,2,1:T(8,128)} %bitcast), calls=%async_computation | async-start | bytes 2097152 | tf_op jit(solution)/shard_map/all_to_all | solution.py:84
where the time goes:
time: 162 us; the launch traced here: 161 us
  matrix products  65 us (40%)
  blocking collectives  31.5 us (19%)
  waiting for transfers between devices  27.1 us (17%)
  starting transfers between devices  25.1 us (15%)
  local copies, waits for them, and re-layouts  7.84 us (5%)
  other arithmetic  3.72 us (2%)
    all_to_all x1, blocking collectives, body(): lax.all_to_all(result[:, None], 'mem', split_axis=0, concat_axis=1, tiled...  31.5 us
    all_to_all x1, waiting for transfers between devices, body(): lax.all_to_all(blocks, 'mem', split_axis=1, concat_axis=0, tiled=True)  26.9 us
    dot_general x12, matrix products, newton(): jnp.einsum('nij,njk->nik', iter_y, middle, precision=HIGH)  22.8 us
    dot_general x12, matrix products, newton(): jnp.einsum('nij,njk->nik', iter_z, iter_y, precision=HIGH)  14.3 us
    dot_general x12, matrix products, newton(): jnp.einsum('nij,njk->nik', middle, iter_z, precision=HIGH)  13.7 us
    ppermute x1, starting transfers between devices, extended(): lax.ppermute(head, axis, [((i + 1) % count, i) for i in range(count)])  10.4 us
    ppermute x1, starting transfers between devices, extended(): lax.ppermute(tail, axis, [(i, (i + 1) % count) for i in range(count)])  8.27 us
    all_to_all x1, starting transfers between devices, body(): lax.all_to_all(blocks, 'mem', split_axis=1, concat_axis=0, tiled=True)  6.47 us
  transfers between devices with their start and end apart: 3, of which 2 were waited for; matrix products, arithmetic and copies ran while one was open for 1% of the time, Pallas kernels for 0%

commit v1 on v0

v1 whole, which is shorter than its diff:
```python
import functools
import math

import jax
import jax.numpy as jnp
from jax import lax
from jax.experimental import pallas as pl
from jax.experimental.pallas import tpu as pltpu
from jax.sharding import PartitionSpec as P

ITERS = 12
F32 = jnp.float32
BF16 = jnp.bfloat16
MESH = pl.DeviceIdType.MESH


def split2(a):
    high = a.astype(BF16)
    return high, (a - high.astype(F32)).astype(BF16)


def split3(a):
    high = a.astype(BF16)
    rest = a - high.astype(F32)
    middle = rest.astype(BF16)
    return high, middle, (rest - middle.astype(F32)).astype(BF16)


def dot(a, b):
    return jnp.dot(a, b, preferred_element_type=F32)


def dot_nt(a, b):
    return lax.dot_general(a, b, (((1,), (1,)), ((), ())), preferred_element_type=F32)


def product(a, b):
    return dot(a[0], b[0]) + (dot(a[0], b[1]) + dot(a[1], b[0]))


def advance(left, middle, right, diffusion, advection):
    return middle + diffusion * (left - 2.0 * middle + right) + advection * (0.5 * (left - right))


def observe(where, count, value, rinv, entries):
    slots = where.shape[1]
    mask = (lax.broadcasted_iota(jnp.int32, (1, slots), 1) < count).astype(F32)
    weight = rinv * mask
    terms = split3(weight) + split3(weight * value)
    row = lax.broadcasted_iota(jnp.int32, (8, slots), 0)
    stacked = jnp.zeros((8, slots), F32)
    for index, term in enumerate(terms):
        stacked = jnp.where(row == index, term.astype(F32), stacked)
    onehot = (lax.broadcasted_iota(jnp.int32, (entries, slots), 0) == where).astype(F32)
    return dot_nt(stacked.astype(BF16), onehot.astype(BF16))


def analyse(states, obs, w_ref, c_ref, members):
    precision = obs[0:1] + (obs[1:2] + obs[2:3])
    target = obs[3:4] + (obs[4:5] + obs[5:6])
    mean = jnp.sum(states, axis=0, keepdims=True) * (1.0 / members)
    anomaly = states - mean
    pull = target - precision * mean
    left = split3(anomaly * precision)
    right = split3(anomaly)
    gram = dot_nt(left[0], right[0]) + (
        (dot_nt(left[0], right[1]) + dot_nt(left[1], right[0]))
        + (dot_nt(left[0], right[2]) + dot_nt(left[2], right[0]) + dot_nt(left[1], right[1]))
    )
    diagonal = lax.broadcasted_iota(jnp.int32, gram.shape, 0) == lax.broadcasted_iota(jnp.int32, gram.shape, 1)
    gram = gram + jnp.where(diagonal, members - 1.0, 0.0)
    square = jnp.sum(jnp.sum(gram * gram, axis=0, keepdims=True), axis=1, keepdims=True)
    scale = jnp.sqrt(square)
    w_ref[...] = gram * (1.0 / scale)
    c_ref[...] = anomaly

    def newton(step, carry):
        iter_w = w_ref[...]
        iter_c = c_ref[...]
        w = split2(iter_w)
        p = 1.5 * iter_w - 0.5 * product(w, w)
        c_ref[...] = 1.5 * iter_c - 0.5 * product(w, split2(iter_c))
        w_ref[...] = 1.5 * p - 0.5 * product(split2(p), w)
        return carry

    lax.fori_loop(0, ITERS - 1, newton, 0)
    iter_c = c_ref[...]
    final = 1.5 * iter_c - 0.5 * product(split2(w_ref[...]), split2(iter_c))
    inner = jnp.sum(final * pull, axis=1, keepdims=True)
    shift = jnp.sum(final * inner, axis=0, keepdims=True) * (1.0 / scale)
    coefficient = math.sqrt(members - 1.0) / jnp.sqrt(scale)
    return (mean + shift) + coefficient * final


def kernel(
    groups, tiles, bg_ref, diff_ref, adv_ref, where_ref, count_ref, value_ref, rinv_ref, out_ref,
    ext, sent, owned, result, obs, w_ref, c_ref,
    load_sem, halo_send, halo_recv, gather_send, gather_recv, back_send, back_recv,
):
    me = lax.axis_index("mem")
    tile = lax.axis_index("tile")
    cols, local, entries = sent.shape
    chunks = cols // groups
    members = groups * local
    right, left = lax.rem(tile + 1, tiles), lax.rem(tile + tiles - 1, tiles)

    load = pltpu.make_async_copy(bg_ref, ext.at[pl.ds(2, cols)], load_sem)
    load.start()
    barrier = pltpu.get_barrier_semaphore()

    def greet(step, carry):
        peer = lax.rem(me + step, groups)
        pl.semaphore_signal(barrier, inc=1, device_id={"mem": peer}, device_id_type=MESH)
        return carry

    lax.fori_loop(1, groups, greet, 0)
    for neighbour in (left, right):
        pl.semaphore_signal(barrier, inc=1, device_id={"tile": neighbour}, device_id_type=MESH)
    diffusion = diff_ref[...]
    advection = adv_ref[...]
    load.wait()
    pl.semaphore_wait(barrier, groups + 1)

    tail = pltpu.make_async_remote_copy(
        src_ref=ext.at[pl.ds(cols, 2)], dst_ref=ext.at[pl.ds(0, 2)], send_sem=halo_send.at[0], recv_sem=halo_recv.at[0],
        device_id={"tile": right}, device_id_type=MESH)
    head = pltpu.make_async_remote_copy(
        src_ref=ext.at[pl.ds(2, 2)], dst_ref=ext.at[pl.ds(cols + 2, 2)], send_sem=halo_send.at[1], recv_sem=halo_recv.at[1],
        device_id={"tile": left}, device_id_type=MESH)
    tail.start()
    head.start()

    def forecast(chunk):
        base = chunk * groups
        width = min(8, groups)
        for start in range(base, base + groups, width):
            cells = ext[start:start + width + 4]
            half = advance(cells[:-2], cells[1:-1], cells[2:], diffusion, advection)
            sent[start:start + width] = advance(half[:-2], half[1:-1], half[2:], diffusion, advection)

    mine = pl.ds(pl.multiple_of(me * local, local), local)

    def scatter(chunk):
        owned[chunk, mine, :] = sent[chunk * groups + me]

        def send(step, carry):
            peer = lax.rem(me + step, groups)
            pltpu.make_async_remote_copy(
                src_ref=sent.at[chunk * groups + peer], dst_ref=owned.at[chunk, mine],
                send_sem=gather_send.at[chunk], recv_sem=gather_recv.at[chunk],
                device_id={"mem": peer}, device_id_type=MESH).start()
            return carry

        lax.fori_loop(1, groups, send, 0)

    for chunk in range(1, chunks - 1):
        forecast(chunk)
        scatter(chunk)
    tail.wait()
    head.wait()
    for chunk in (chunks - 1, 0):
        forecast(chunk)
        scatter(chunk)

    for chunk in range(chunks):
        row = pl.ds(chunk * groups + me, 1)
        lanes = lax.broadcasted_iota(jnp.int32, count_ref.shape, 1)
        count = jnp.sum(jnp.where(lanes == chunk * groups + me, count_ref[...], 0), axis=1, keepdims=True)
        obs[chunk] = observe(where_ref[row, :], count, value_ref[row, :], rinv_ref[row, :], entries)

    bulk = (groups - 1) * local

    def column(step, carry):
        chunk = lax.rem(step + 1, chunks)
        pltpu.make_async_remote_copy(
            src_ref=owned.at[chunk, pl.ds(0, bulk)], dst_ref=owned.at[chunk, pl.ds(0, bulk)],
            send_sem=gather_send.at[chunk], recv_sem=gather_recv.at[chunk],
            device_id={"mem": me}, device_id_type=MESH).wait_recv()
        result[chunk] = analyse(owned[chunk], obs[chunk], w_ref, c_ref, members)
        at = chunk * groups + me

        def send(hop, inner):
            peer = lax.rem(me + hop, groups)
            pltpu.make_async_remote_copy(
                src_ref=result.at[chunk, pl.ds(pl.multiple_of(peer * local, local), local)], dst_ref=out_ref.at[at],
                send_sem=back_send.at[chunk], recv_sem=back_recv.at[chunk],
                device_id={"mem": peer}, device_id_type=MESH).start()
            return inner

        lax.fori_loop(1, groups, send, 0)
        out_ref[at] = result[chunk, mine, :]
        return carry

    lax.fori_loop(0, chunks, column, 0)
    for chunk in range(chunks):
        pltpu.make_async_remote_copy(
            src_ref=owned.at[chunk, pl.ds(0, bulk)], dst_ref=owned.at[chunk, pl.ds(0, bulk)],
            send_sem=gather_send.at[chunk], recv_sem=gather_recv.at[chunk],
            device_id={"mem": me}, device_id_type=MESH).wait_send()
        pltpu.make_async_remote_copy(
            src_ref=out_ref.at[pl.ds(0, groups - 1)], dst_ref=out_ref.at[pl.ds(0, groups - 1)],
            send_sem=back_send.at[chunk], recv_sem=back_recv.at[chunk],
            device_id={"mem": me}, device_id_type=MESH).wait()


def body(groups, tiles, background, diffusion, advection, obs_where, obs_count, obs_value, obs_rinv):
    local, cols, entries = background.shape
    chunks = cols // groups
    members = local * groups
    vmem = pl.BlockSpec(memory_space=pltpu.VMEM)
    result = pl.pallas_call(
        functools.partial(kernel, groups, tiles),
        out_shape=jax.ShapeDtypeStruct((cols, local, entries), F32),
        in_specs=[pl.BlockSpec(memory_space=pl.ANY)] + [vmem] * 6,
        out_specs=vmem,
        scratch_shapes=[
            pltpu.VMEM((cols + 4, local, entries), F32),
            pltpu.VMEM((cols, local, entries), F32),
            pltpu.VMEM((chunks, members, entries), F32),
            pltpu.VMEM((chunks, members, entries), F32),
            pltpu.VMEM((chunks, 8, entries), F32),
            pltpu.VMEM((members, members), F32),
            pltpu.VMEM((members, entries), F32),
            pltpu.SemaphoreType.DMA,
            pltpu.SemaphoreType.DMA((2,)),
            pltpu.SemaphoreType.DMA((2,)),
            pltpu.SemaphoreType.DMA((chunks,)),
            pltpu.SemaphoreType.DMA((chunks,)),
            pltpu.SemaphoreType.DMA((chunks,)),
            pltpu.SemaphoreType.DMA((chunks,)),
        ],
        compiler_params=pltpu.CompilerParams(collective_id=0, has_side_effects=True, vmem_limit_bytes=48 << 20),
    )(
        jnp.transpose(background, (1, 0, 2)), diffusion[None, :], advection[None, :],
        obs_where[0], obs_count, obs_value[0], obs_rinv[0],
    )
    return jnp.transpose(result, (1, 0, 2))


def solution(mesh):
    return jax.shard_map(
        functools.partial(body, mesh.shape["mem"], mesh.shape["tile"]),
        mesh=mesh,
        in_specs=(
            P("mem", "tile", None),
            P(),
            P(),
            P("tile", None, None),
            P("tile", None),
            P("tile", None, None),
            P("tile", None, None),
        ),
        out_specs=P("mem", "tile", None),
        check_vma=False,
    )
```

time: 162 us -> 69.8 us (0.43)
  Pallas kernels: 0 us -> 65.7 us
  matrix products: 65 us -> 0 us
  blocking collectives: 31.5 us -> 0 us
  waiting for transfers between devices: 27.1 us -> 0 us
  starting transfers between devices: 25.1 us -> 0 us
  local copies, waits for them, and re-layouts: 7.84 us -> 3.84 us
  other arithmetic: 3.72 us -> 0 us
    pallas_call x0 -> x1, Pallas kernels: none -> 65.7 us  [body(): pl.pallas_call(functools.partial(kernel, groups, tiles), out_shape=jax.Sh...]
    dot_general x43 -> x0, matrix products: 65 us -> none  [the longest x12 22.8 us: newton(): jnp.einsum('nij,njk->nik', iter_y, middle, precision=HIGH)]
    all_to_all x1 -> x0, blocking collectives: 31.5 us -> none  [body(): lax.all_to_all(result[:, None], 'mem', split_axis=0, concat_axis=1, tiled...]
    all_to_all x1 -> x0, waiting for transfers between devices: 26.9 us -> none  [body(): lax.all_to_all(blocks, 'mem', split_axis=1, concat_axis=0, tiled=True)]
    ppermute x2 -> x0, starting transfers between devices: 18.7 us -> none  [the longest x1 10.4 us: extended(): lax.ppermute(head, axis, [((i + 1) % count, i) for i in range(count)])]
    all_to_all x1 -> x0, starting transfers between devices: 6.47 us -> none  [body(): lax.all_to_all(blocks, 'mem', split_axis=1, concat_axis=0, tiled=True)]
    while x24 -> x0, local copies, waits for them, and re-layouts: 1.76 us -> none
  transfers between devices with their start and end apart: 3 -> 0, of which waited for: 2 -> 0; matrix products, arithmetic and copies ran while one was open for 1% -> 0% of each run, Pallas kernels for 0% -> 0%
where the time goes in v1:
time: 69.8 us; the launch traced here: 69.7 us
  Pallas kernels  65.7 us (94%)
  local copies, waits for them, and re-layouts  3.84 us (6%)
    pallas_call x1, Pallas kernels, body(): pl.pallas_call(functools.partial(kernel, groups, tiles), out_shape=jax.Sh...  65.7 us
    unnamed x13, local copies, waits for them, and re-layouts  2.55 us

profile of v1, /device:TPU:1, one launch (start us, length us, event | category | flops | bytes accessed | tf_op | source)
XLA Modules:
  0.0 69.7 jit_solution(4031702925169345943)
XLA Ops:
  0.0 0.0 copy-start
  0.0 0.0 copy-start.1
  0.0 0.0 copy-start.2
  0.0 0.0 copy-start.4
  0.0 1.9 %copy.11 = f32[8,128,256]{2,0,1:T(8,128)S(1)} copy(f32[8,128,256]{2,1,0:T(8,128)} %param.7) | data formatting | bytes 2097152 | tf_op args[0]
  1.9 0.0 copy-start.3
  1.9 0.0 copy-start.5
  2.0 0.0 copy-done
  2.0 0.0 copy-done.1
  2.0 0.0 copy-done.2
  2.0 0.0 copy-done.4
  2.0 0.6 copy-done.3
  2.6 0.0 copy-done.5
  2.6 65.7 %shard_map.73 = f32[128,8,256]{2,1,0:T(8,128)S(1)} custom-call(f32[128,8,256]{2,1,0:T(8,128)S(1)} %bitcast.10, f32[1,256]{1,0:T(1,128)S(1)} %bitcast.14, f32[1,256]{1,0:T(1,128)S(1)} %bitcast.15, s32[128,512]{1,0:T(8,128)S(1)} %bitcast.11, s32[1,128]{1,0:T(1,128)S(1)} %copy-done.5, f32[128,512]{1,0:T(8,128)S(1)} %bitcast.12, f32[128,512]{1,0:T(8,128)S(1)} %bitcast.13), custom_call_target="tpu_custom_call" | custom-call | tf_op jit(solution)/shard_map/pallas_call | solution.py:211
  68.4 1.3 %copy.9 = f32[8,128,256]{2,1,0:T(8,128)} copy(f32[8,128,256]{2,0,1:T(8,128)S(1)} %bitcast.9) | data formatting | bytes 2097152 | tf_op jit(solution)/shard_map/transpose | solution.py:237
Async XLA Ops:
  0.0 2.0 %copy-start = (s32[1,128,512]{2,1,0:T(8,128)S(1)}, s32[1,128,512]{2,1,0:T(8,128)}, u32[]{:S(2)}) copy-start(s32[1,128,512]{2,1,0:T(8,128)} %param.10) | copy-start | bytes 786436
  0.0 2.0 %copy-start.1 = (f32[1,128,512]{2,1,0:T(8,128)S(1)}, f32[1,128,512]{2,1,0:T(8,128)}, u32[]{:S(2)}) copy-start(f32[1,128,512]{2,1,0:T(8,128)} %param.12) | copy-start | bytes 786436
  0.0 2.0 %copy-start.2 = (f32[1,128,512]{2,1,0:T(8,128)S(1)}, f32[1,128,512]{2,1,0:T(8,128)}, u32[]{:S(2)}) copy-start(f32[1,128,512]{2,1,0:T(8,128)} %param.13) | copy-start | bytes 786436
  0.0 2.0 %copy-start.4 = (f32[256]{0:T(256)S(1)}, f32[256]{0:T(256)}, u32[]{:S(2)}) copy-start(f32[256]{0:T(256)} %param.9) | copy-start | bytes 3076
  1.9 0.7 copy-start.3
  1.9 0.7 copy-start.5

commit v2 on v1

--- a/solution.py
+++ b/solution.py
@@ -92,10 +92,13 @@
     return (mean + shift) + coefficient * final
 
 
+ZERO, HEAD, TILE, LATE = 0, 1, 2, 3
+
+
 def kernel(
     groups, tiles, bg_ref, diff_ref, adv_ref, where_ref, count_ref, value_ref, rinv_ref, out_ref,
-    ext, sent, owned, result, obs, w_ref, c_ref,
-    load_sem, halo_send, halo_recv, gather_send, gather_recv, back_send, back_recv,
+    ext, sent, owned, result, obs, where, value, rinv, diff, adv, counts, w_ref, c_ref,
+    load_sem, halo_send, halo_recv, gather_send, gather_recv, back_send, back_recv, go_sem, first_sem, tile_sem,
 ):
     me = lax.axis_index("mem")
     tile = lax.axis_index("tile")
@@ -104,22 +107,113 @@
     members = groups * local
     right, left = lax.rem(tile + 1, tiles), lax.rem(tile + tiles - 1, tiles)
 
-    load = pltpu.make_async_copy(bg_ref, ext.at[pl.ds(2, cols)], load_sem)
-    load.start()
+    loads = [
+        pltpu.make_async_copy(bg_ref.at[index], ext.at[pl.ds(2, cols), index], load_sem.at[index])
+        for index in range(local)
+    ]
+    small = ((diff_ref, diff), (adv_ref, adv), (count_ref, counts), (where_ref, where), (value_ref, value), (rinv_ref, rinv))
+    loads += [
+        pltpu.make_async_copy(source, target, load_sem.at[local + index]) for index, (source, target) in enumerate(small)
+    ]
+    for load in loads:
+        load.start()
     barrier = pltpu.get_barrier_semaphore()
 
-    def greet(step, carry):
-        peer = lax.rem(me + step, groups)
-        pl.semaphore_signal(barrier, inc=1, device_id={"mem": peer}, device_id_type=MESH)
-        return carry
-
-    lax.fori_loop(1, groups, greet, 0)
-    for neighbour in (left, right):
-        pl.semaphore_signal(barrier, inc=1, device_id={"tile": neighbour}, device_id_type=MESH)
-    diffusion = diff_ref[...]
-    advection = adv_ref[...]
-    load.wait()
-    pl.semaphore_wait(barrier, groups + 1)
+    def peers(action):
+        def visit(step, carry):
+            action(lax.rem(me + step, groups))
+            return carry
+
+        lax.fori_loop(1, groups, visit, 0)
+
+    def tell(semaphore, peer, **where_to):
+        pl.semaphore_signal(semaphore, inc=1, device_id={"mem": peer, **where_to}, device_id_type=MESH)
+
+    @pl.when(me == ZERO)
+    def _():
+        tell(barrier, LATE)
+
+    @pl.when(me != ZERO)
+    def _():
+        peers(lambda peer: pl.when((peer == HEAD) | (peer > LATE))(lambda: tell(barrier, peer)))
+
+    @pl.when((me == HEAD) | (me > LATE))
+    def _():
+        pl.semaphore_wait(barrier, groups - 2)
+
+    @pl.when(me == HEAD)
+    def _():
+        tell(go_sem, TILE)
+        tell(go_sem, LATE)
+
+    @pl.when((me == TILE) | (me == LATE))
+    def _():
+        pl.semaphore_wait(go_sem, 1)
+
+    @pl.when(me == ZERO)
+    def _():
+        pl.semaphore_wait(first_sem, 1)
+
+    for load in loads[:local + 2]:
+        load.wait()
+    diffusion = diff[...]
+    advection = adv[...]
+
+    def forecast(begin, end):
+        width = min(8, groups)
+        for start in range(begin, end, width):
+            stop = min(start + width, end)
+            cells = ext[start:stop + 4]
+            half = advance(cells[:-2], cells[1:-1], cells[2:], diffusion, advection)
+            sent[start:stop] = advance(half[:-2], half[1:-1], half[2:], diffusion, advection)
+
+    mine = pl.ds(pl.multiple_of(me * local, local), local)
+
+    def hand_over(chunk, peer):
+        pltpu.make_async_remote_copy(
+            src_ref=sent.at[chunk * groups + peer], dst_ref=owned.at[chunk, mine],
+            send_sem=gather_send.at[chunk], recv_sem=gather_recv.at[chunk],
+            device_id={"mem": peer}, device_id_type=MESH).start()
+
+    def keep(chunk):
+        owned[chunk, mine, :] = sent[chunk * groups + me]
+
+    last = chunks - 1
+    forecast(groups, 2 * groups)
+    keep(1)
+    peers(lambda peer: pl.when(peer != ZERO)(lambda: hand_over(1, peer)))
+
+    @pl.when(me == LATE)
+    def _():
+        pl.semaphore_wait(barrier, 1)
+        peers(lambda peer: tell(first_sem, peer))
+        tell(barrier, TILE, tile=left)
+        tell(barrier, TILE, tile=right)
+
+    @pl.when((me != LATE) & (me != ZERO))
+    def _():
+        pl.semaphore_wait(first_sem, 1)
+
+    @pl.when(me != ZERO)
+    def _():
+        hand_over(1, ZERO)
+
+    for chunk in range(2, last):
+        forecast(chunk * groups, (chunk + 1) * groups)
+        keep(chunk)
+        peers(lambda peer: hand_over(chunk, peer))
+    forecast(last * groups, cols - 2)
+    peers(lambda peer: pl.when(peer < groups - 2)(lambda: hand_over(last, peer)))
+    forecast(2, groups)
+    peers(lambda peer: pl.when(peer > 1)(lambda: hand_over(0, peer)))
+
+    for load in loads[local + 2:]:
+        load.wait()
+    for chunk in range(chunks):
+        row = pl.ds(chunk * groups + me, 1)
+        lanes = lax.broadcasted_iota(jnp.int32, counts.shape, 1)
+        count = jnp.sum(jnp.where(lanes == chunk * groups + me, counts[...], 0), axis=1, keepdims=True)
+        obs[chunk] = observe(where[row, :], count, value[row, :], rinv[row, :], entries)
 
     tail = pltpu.make_async_remote_copy(
         src_ref=ext.at[pl.ds(cols, 2)], dst_ref=ext.at[pl.ds(0, 2)], send_sem=halo_send.at[0], recv_sem=halo_recv.at[0],
@@ -127,68 +221,47 @@
     head = pltpu.make_async_remote_copy(
         src_ref=ext.at[pl.ds(2, 2)], dst_ref=ext.at[pl.ds(cols + 2, 2)], send_sem=halo_send.at[1], recv_sem=halo_recv.at[1],
         device_id={"tile": left}, device_id_type=MESH)
-    tail.start()
-    head.start()
-
-    def forecast(chunk):
-        base = chunk * groups
-        width = min(8, groups)
-        for start in range(base, base + groups, width):
-            cells = ext[start:start + width + 4]
-            half = advance(cells[:-2], cells[1:-1], cells[2:], diffusion, advection)
-            sent[start:start + width] = advance(half[:-2], half[1:-1], half[2:], diffusion, advection)
-
-    mine = pl.ds(pl.multiple_of(me * local, local), local)
-
-    def scatter(chunk):
-        owned[chunk, mine, :] = sent[chunk * groups + me]
-
-        def send(step, carry):
-            peer = lax.rem(me + step, groups)
-            pltpu.make_async_remote_copy(
-                src_ref=sent.at[chunk * groups + peer], dst_ref=owned.at[chunk, mine],
-                send_sem=gather_send.at[chunk], recv_sem=gather_recv.at[chunk],
-                device_id={"mem": peer}, device_id_type=MESH).start()
-            return carry
-
-        lax.fori_loop(1, groups, send, 0)
-
-    for chunk in range(1, chunks - 1):
-        forecast(chunk)
-        scatter(chunk)
-    tail.wait()
-    head.wait()
-    for chunk in (chunks - 1, 0):
-        forecast(chunk)
-        scatter(chunk)
-
-    for chunk in range(chunks):
-        row = pl.ds(chunk * groups + me, 1)
-        lanes = lax.broadcasted_iota(jnp.int32, count_ref.shape, 1)
-        count = jnp.sum(jnp.where(lanes == chunk * groups + me, count_ref[...], 0), axis=1, keepdims=True)
-        obs[chunk] = observe(where_ref[row, :], count, value_ref[row, :], rinv_ref[row, :], entries)
+
+    def exchange_edges():
+        @pl.when(me == TILE)
+        def _():
+            pl.semaphore_wait(barrier, 2)
+            peers(lambda peer: tell(tile_sem, peer))
+
+        @pl.when(me != TILE)
+        def _():
+            pl.semaphore_wait(tile_sem, 1)
+
+        tail.start()
+        head.start()
+
+    def send_edges():
+        tail.wait()
+        head.wait()
+        forecast(0, 2)
+        forecast(cols - 2, cols)
+        keep(0)
+        keep(last)
+        for chunk, owner in ((last, groups - 2), (last, groups - 1), (0, 0), (0, 1)):
+            pl.when(me != owner)(functools.partial(hand_over, chunk, owner))
 
     bulk = (groups - 1) * local
 
     def column(step, carry):
         chunk = lax.rem(step + 1, chunks)
+        pl.when(step == 2)(send_edges)
         pltpu.make_async_remote_copy(
             src_ref=owned.at[chunk, pl.ds(0, bulk)], dst_ref=owned.at[chunk, pl.ds(0, bulk)],
             send_sem=gather_send.at[chunk], recv_sem=gather_recv.at[chunk],
             device_id={"mem": me}, device_id_type=MESH).wait_recv()
         result[chunk] = analyse(owned[chunk], obs[chunk], w_ref, c_ref, members)
         at = chunk * groups + me
-
-        def send(hop, inner):
-            peer = lax.rem(me + hop, groups)
-            pltpu.make_async_remote_copy(
-                src_ref=result.at[chunk, pl.ds(pl.multiple_of(peer * local, local), local)], dst_ref=out_ref.at[at],
-                send_sem=back_send.at[chunk], recv_sem=back_recv.at[chunk],
-                device_id={"mem": peer}, device_id_type=MESH).start()
-            return inner
-
-        lax.fori_loop(1, groups, send, 0)
+        peers(lambda peer: pltpu.make_async_remote_copy(
+            src_ref=result.at[chunk, pl.ds(pl.multiple_of(peer * local, local), local)], dst_ref=out_ref.at[at],
+            send_sem=back_send.at[chunk], recv_sem=back_recv.at[chunk],
+            device_id={"mem": peer}, device_id_type=MESH).start())
         out_ref[at] = result[chunk, mine, :]
+        pl.when(step == 0)(exchange_edges)
         return carry
 
     lax.fori_loop(0, chunks, column, 0)
@@ -208,10 +281,12 @@
     chunks = cols // groups
     members = local * groups
     vmem = pl.BlockSpec(memory_space=pltpu.VMEM)
+    hbm = pl.BlockSpec(memory_space=pltpu.HBM)
+    slots = obs_where.shape[2]
     result = pl.pallas_call(
         functools.partial(kernel, groups, tiles),
-        out_shape=jax.ShapeDtypeStruct((cols, local, entries), F32),
-        in_specs=[pl.BlockSpec(memory_space=pl.ANY)] + [vmem] * 6,
+        out_shape=pltpu.VMEM((cols, local, entries), F32),
+        in_specs=[hbm] * 7,
         out_specs=vmem,
         scratch_shapes=[
             pltpu.VMEM((cols + 4, local, entries), F32),
@@ -219,21 +294,32 @@
             pltpu.VMEM((chunks, members, entries), F32),
             pltpu.VMEM((chunks, members, entries), F32),
             pltpu.VMEM((chunks, 8, entries), F32),
+            pltpu.VMEM((cols, slots), jnp.int32),
+            pltpu.VMEM((cols, slots), F32),
+            pltpu.VMEM((cols, slots), F32),
+            pltpu.VMEM((1, entries), F32),
+            pltpu.VMEM((1, entries), F32),
+            pltpu.VMEM((1, cols), jnp.int32),
             pltpu.VMEM((members, members), F32),
             pltpu.VMEM((members, entries), F32),
-            pltpu.SemaphoreType.DMA,
+            pltpu.SemaphoreType.DMA((local + 6,)),
             pltpu.SemaphoreType.DMA((2,)),
             pltpu.SemaphoreType.DMA((2,)),
             pltpu.SemaphoreType.DMA((chunks,)),
             pltpu.SemaphoreType.DMA((chunks,)),
             pltpu.SemaphoreType.DMA((chunks,)),
             pltpu.SemaphoreType.DMA((chunks,)),
+            pltpu.SemaphoreType.REGULAR,
+            pltpu.SemaphoreType.REGULAR,
+            pltpu.SemaphoreType.REGULAR,
         ],
         compiler_params=pltpu.CompilerParams(collective_id=0, has_side_effects=True, vmem_limit_bytes=48 << 20),
-    )(
-        jnp.transpose(background, (1, 0, 2)), diffusion[None, :], advection[None, :],
-        obs_where[0], obs_count, obs_value[0], obs_rinv[0],
-    )
+    )(*(
+        pltpu.with_memory_space_constraint(operand, pltpu.HBM)
+        for operand in (
+            background, diffusion[None, :], advection[None, :], obs_where[0], obs_count, obs_value[0], obs_rinv[0],
+        )
+    ))
     return jnp.transpose(result, (1, 0, 2))
 
 

time: 69.8 us -> 71.1 us (1.019)
  the two profiles are of different devices: /device:TPU:1 before, /device:TPU:327 now
where the time goes in v2:
time: 71.1 us; the launch traced here: 71 us
  Pallas kernels  69.7 us (98%)
  local copies, waits for them, and re-layouts  1.29 us (2%)
    pallas_call x1, Pallas kernels, body(): pl.pallas_call(functools.partial(kernel, groups, tiles), out_shape=pltpu....  69.7 us

profile of v2, /device:TPU:327, one launch (start us, length us, event | category | flops | bytes accessed | tf_op | source)
XLA Modules:
  0.0 71.0 jit_solution(2679382751805955356)
XLA Ops:
  0.0 69.7 %shard_map.73 = f32[128,8,256]{2,1,0:T(8,128)S(1)} custom-call(f32[8,128,256]{2,1,0:T(8,128)} %bg_ref.1, f32[1,256]{1,0:T(1,128)} %bitcast.10, f32[1,256]{1,0:T(1,128)} %bitcast.11, s32[128,512]{1,0:T(8,128)} %bitcast.7, s32[1,128]{1,0:T(1,128)} %count_ref.1, f32[128,512]{1,0:T(8,128)} %bitcast.8, f32[128,512]{1,0:T(8,128)} %bitcast.9), custom_call_target="tpu_custom_call" | custom-call | tf_op jit(solution)/shard_map/pallas_call | solution.py:286
  69.7 1.3 %copy.8 = f32[8,128,256]{2,1,0:T(8,128)} copy(f32[8,128,256]{2,0,1:T(8,128)S(1)} %bitcast.6) | data formatting | bytes 2097152 | tf_op jit(solution)/shard_map/transpose | solution.py:323

commit v3 on v2

--- a/solution.py
+++ b/solution.py
@@ -249,7 +249,8 @@
 
     def column(step, carry):
         chunk = lax.rem(step + 1, chunks)
-        pl.when(step == 2)(send_edges)
+        chunk = jnp.where((me >= groups // 2) & (step >= last - 1), (step - (last - 1)) * last, chunk)
+        pl.when(step == last - 1)(send_edges)
         pltpu.make_async_remote_copy(
             src_ref=owned.at[chunk, pl.ds(0, bulk)], dst_ref=owned.at[chunk, pl.ds(0, bulk)],
             send_sem=gather_send.at[chunk], recv_sem=gather_recv.at[chunk],
@@ -261,9 +262,10 @@
             send_sem=back_send.at[chunk], recv_sem=back_recv.at[chunk],
             device_id={"mem": peer}, device_id_type=MESH).start())
         out_ref[at] = result[chunk, mine, :]
-        pl.when(step == 0)(exchange_edges)
+        pl.when((step == 0) & (tile == 0))(exchange_edges)
         return carry
 
+    pl.when(tile != 0)(exchange_edges)
     lax.fori_loop(0, chunks, column, 0)
     for chunk in range(chunks):
         pltpu.make_async_remote_copy(

time: 71.1 us -> 63.8 us (0.90)
  the two profiles are of different devices: /device:TPU:327 before, /device:TPU:199 now
where the time goes in v3:
time: 63.8 us; the launch traced here: 63.7 us
  Pallas kernels  62.4 us (98%)
  local copies, waits for them, and re-layouts  1.29 us (2%)
    pallas_call x1, Pallas kernels, body(): pl.pallas_call(functools.partial(kernel, groups, tiles), out_shape=pltpu....  62.4 us
    transpose x1, local copies, waits for them, and re-layouts, body(): return jnp.transpose(result, (1, 0, 2))  1.29 us

profile of v3, /device:TPU:199, one launch (start us, length us, event | category | flops | bytes accessed | tf_op | source)
XLA Modules:
  0.0 63.7 jit_solution(9517596738140649027)
XLA Ops:
  0.0 62.4 %shard_map.73 = f32[128,8,256]{2,1,0:T(8,128)S(1)} custom-call(f32[8,128,256]{2,1,0:T(8,128)} %bg_ref.1, f32[1,256]{1,0:T(1,128)} %bitcast.10, f32[1,256]{1,0:T(1,128)} %bitcast.11, s32[128,512]{1,0:T(8,128)} %bitcast.7, s32[1,128]{1,0:T(1,128)} %count_ref.1, f32[128,512]{1,0:T(8,128)} %bitcast.8, f32[128,512]{1,0:T(8,128)} %bitcast.9), custom_call_target="tpu_custom_call" | custom-call | tf_op jit(solution)/shard_map/pallas_call | solution.py:288
  62.4 1.3 %copy.8 = f32[8,128,256]{2,1,0:T(8,128)} copy(f32[8,128,256]{2,0,1:T(8,128)S(1)} %bitcast.6) | data formatting | bytes 2097152 | tf_op jit(solution)/shard_map/transpose | solution.py:325

commit v4 on v3

--- a/solution.py
+++ b/solution.py
@@ -55,7 +55,7 @@
     return dot_nt(stacked.astype(BF16), onehot.astype(BF16))
 
 
-def analyse(states, obs, w_ref, c_ref, members):
+def analyse(states, obs, w_ref, c_ref, s_ref, members, halfway):
     precision = obs[0:1] + (obs[1:2] + obs[2:3])
     target = obs[3:4] + (obs[4:5] + obs[5:6])
     mean = jnp.sum(states, axis=0, keepdims=True) * (1.0 / members)
@@ -74,16 +74,24 @@
     w_ref[...] = gram * (1.0 / scale)
     c_ref[...] = anomaly
 
+    half = members // 2
+    strips = (slice(0, half), slice(half, members))
+
     def newton(step, carry):
-        iter_w = w_ref[...]
+        w = split2(w_ref[...])
+        s_ref[0], s_ref[1] = w
+        p = [1.5 * w_ref[rows] - 0.5 * product((s_ref[0, rows], s_ref[1, rows]), w) for rows in strips]
         iter_c = c_ref[...]
-        w = split2(iter_w)
-        p = 1.5 * iter_w - 0.5 * product(w, w)
-        c_ref[...] = 1.5 * iter_c - 0.5 * product(w, split2(iter_c))
-        w_ref[...] = 1.5 * p - 0.5 * product(split2(p), w)
+        c = split2(iter_c)
+        for rows in strips:
+            c_ref[rows] = 1.5 * iter_c[rows] - 0.5 * product((s_ref[0, rows], s_ref[1, rows]), c)
+        for rows, part in zip(strips, p):
+            w_ref[rows] = 1.5 * part - 0.5 * product(split2(part), w)
         return carry
 
-    lax.fori_loop(0, ITERS - 1, newton, 0)
+    lax.fori_loop(0, ITERS // 2, newton, 0)
+    halfway()
+    lax.fori_loop(ITERS // 2, ITERS - 1, newton, 0)
     iter_c = c_ref[...]
     final = 1.5 * iter_c - 0.5 * product(split2(w_ref[...]), split2(iter_c))
     inner = jnp.sum(final * pull, axis=1, keepdims=True)
@@ -97,7 +105,7 @@
 
 def kernel(
     groups, tiles, bg_ref, diff_ref, adv_ref, where_ref, count_ref, value_ref, rinv_ref, out_ref,
-    ext, sent, owned, result, obs, where, value, rinv, diff, adv, counts, w_ref, c_ref,
+    ext, sent, owned, result, obs, where, value, rinv, diff, adv, counts, w_ref, c_ref, s_ref,
     load_sem, halo_send, halo_recv, gather_send, gather_recv, back_send, back_recv, go_sem, first_sem, tile_sem,
 ):
     me = lax.axis_index("mem")
@@ -115,16 +123,35 @@
     loads += [
         pltpu.make_async_copy(source, target, load_sem.at[local + index]) for index, (source, target) in enumerate(small)
     ]
-    for load in loads:
-        load.start()
     barrier = pltpu.get_barrier_semaphore()
+
+    strip, side = lax.div(me, 8), lax.rem(lax.div(me, 4), 2)
+    lows = [lax.rem(me + index, 4) for index in range(4)]
 
     def peers(action):
         def visit(step, carry):
             action(lax.rem(me + step, groups))
             return carry
 
-        lax.fori_loop(1, groups, visit, 0)
+        def block(base, begin, index):
+            first = base + 8 * lax.rem(strip + index, 4)
+            for low in lows[begin:]:
+                action(first + low)
+
+        def far(index, carry):
+            block(4 * (1 - side), 0, index)
+            return carry
+
+        def near(index, carry):
+            block(4 * side, 0, index)
+            return carry
+
+        if groups != 32:
+            lax.fori_loop(1, groups, visit, 0)
+        else:
+            lax.fori_loop(0, 4, far, 0)
+            block(4 * side, 1, 0)
+            lax.fori_loop(1, 4, near, 0)
 
     def tell(semaphore, peer, **where_to):
         pl.semaphore_signal(semaphore, inc=1, device_id={"mem": peer, **where_to}, device_id_type=MESH)
@@ -136,6 +163,9 @@
     @pl.when(me != ZERO)
     def _():
         peers(lambda peer: pl.when((peer == HEAD) | (peer > LATE))(lambda: tell(barrier, peer)))
+
+    for load in loads:
+        load.start()
 
     @pl.when((me == HEAD) | (me > LATE))
     def _():
@@ -203,9 +233,37 @@
         keep(chunk)
         peers(lambda peer: hand_over(chunk, peer))
     forecast(last * groups, cols - 2)
+    forecast(2, groups)
+
+    tail = pltpu.make_async_remote_copy(
+        src_ref=ext.at[pl.ds(cols, 2)], dst_ref=ext.at[pl.ds(0, 2)], send_sem=halo_send.at[0], recv_sem=halo_recv.at[0],
+        device_id={"tile": right}, device_id_type=MESH)
+    head = pltpu.make_async_remote_copy(
+        src_ref=ext.at[pl.ds(2, 2)], dst_ref=ext.at[pl.ds(cols + 2, 2)], send_sem=halo_send.at[1], recv_sem=halo_recv.at[1],
+        device_id={"tile": left}, device_id_type=MESH)
+
+    def announce():
+        @pl.when(me == TILE)
+        def _():
+            pl.semaphore_wait(barrier, 2)
+            peers(lambda peer: tell(tile_sem, peer))
+
+    def exchange_edges():
+        @pl.when(me != TILE)
+        def _():
+            pl.semaphore_wait(tile_sem, 1)
+
+        tail.start()
+        head.start()
+
+    @pl.when(tile != 0)
+    def _():
+        announce()
+        exchange_edges()
+
     peers(lambda peer: pl.when(peer < groups - 2)(lambda: hand_over(last, peer)))
-    forecast(2, groups)
     peers(lambda peer: pl.when(peer > 1)(lambda: hand_over(0, peer)))
+
 
     for load in loads[local + 2:]:
         load.wait()
@@ -214,26 +272,6 @@
         lanes = lax.broadcasted_iota(jnp.int32, counts.shape, 1)
         count = jnp.sum(jnp.where(lanes == chunk * groups + me, counts[...], 0), axis=1, keepdims=True)
         obs[chunk] = observe(where[row, :], count, value[row, :], rinv[row, :], entries)
-
-    tail = pltpu.make_async_remote_copy(
-        src_ref=ext.at[pl.ds(cols, 2)], dst_ref=ext.at[pl.ds(0, 2)], send_sem=halo_send.at[0], recv_sem=halo_recv.at[0],
-        device_id={"tile": right}, device_id_type=MESH)
-    head = pltpu.make_async_remote_copy(
-        src_ref=ext.at[pl.ds(2, 2)], dst_ref=ext.at[pl.ds(cols + 2, 2)], send_sem=halo_send.at[1], recv_sem=halo_recv.at[1],
-        device_id={"tile": left}, device_id_type=MESH)
-
-    def exchange_edges():
-        @pl.when(me == TILE)
-        def _():
-            pl.semaphore_wait(barrier, 2)
-            peers(lambda peer: tell(tile_sem, peer))
-
-        @pl.when(me != TILE)
-        def _():
-            pl.semaphore_wait(tile_sem, 1)
-
-        tail.start()
-        head.start()
 
     def send_edges():
         tail.wait()
@@ -250,22 +288,25 @@
     def column(step, carry):
         chunk = lax.rem(step + 1, chunks)
         chunk = jnp.where((me >= groups // 2) & (step >= last - 1), (step - (last - 1)) * last, chunk)
-        pl.when(step == last - 1)(send_edges)
         pltpu.make_async_remote_copy(
             src_ref=owned.at[chunk, pl.ds(0, bulk)], dst_ref=owned.at[chunk, pl.ds(0, bulk)],
             send_sem=gather_send.at[chunk], recv_sem=gather_recv.at[chunk],
             device_id={"mem": me}, device_id_type=MESH).wait_recv()
-        result[chunk] = analyse(owned[chunk], obs[chunk], w_ref, c_ref, members)
+        pl.when((step == 0) & (tile == 0))(announce)
+
+        def halfway():
+            pl.when((step == 0) & (tile == 0))(exchange_edges)
+            pl.when(step == 1)(send_edges)
+
+        result[chunk] = analyse(owned[chunk], obs[chunk], w_ref, c_ref, s_ref, members, halfway)
         at = chunk * groups + me
         peers(lambda peer: pltpu.make_async_remote_copy(
             src_ref=result.at[chunk, pl.ds(pl.multiple_of(peer * local, local), local)], dst_ref=out_ref.at[at],
             send_sem=back_send.at[chunk], recv_sem=back_recv.at[chunk],
             device_id={"mem": peer}, device_id_type=MESH).start())
         out_ref[at] = result[chunk, mine, :]
-        pl.when((step == 0) & (tile == 0))(exchange_edges)
         return carry
 
-    pl.when(tile != 0)(exchange_edges)
     lax.fori_loop(0, chunks, column, 0)
     for chunk in range(chunks):
         pltpu.make_async_remote_copy(
@@ -304,6 +345,7 @@
             pltpu.VMEM((1, cols), jnp.int32),
             pltpu.VMEM((members, members), F32),
             pltpu.VMEM((members, entries), F32),
+            pltpu.VMEM((2, members, members), BF16),
             pltpu.SemaphoreType.DMA((local + 6,)),
             pltpu.SemaphoreType.DMA((2,)),
             pltpu.SemaphoreType.DMA((2,)),

time: 63.8 us -> 62.3 us (0.976)
  the two profiles are of different devices: /device:TPU:199 before, /device:TPU:1 now
where the time goes in v4:
time: 62.3 us; the launch traced here: 62.2 us
  Pallas kernels  60.9 us (98%)
  local copies, waits for them, and re-layouts  1.29 us (2%)
    pallas_call x1, Pallas kernels, body(): pl.pallas_call(functools.partial(kernel, groups, tiles), out_shape=pltpu....  60.9 us
    transpose x1, local copies, waits for them, and re-layouts, body(): return jnp.transpose(result, (1, 0, 2))  1.29 us

profile of v4, /device:TPU:1, one launch (start us, length us, event | category | flops | bytes accessed | tf_op | source)
XLA Modules:
  0.0 62.2 jit_solution(15005716413292642991)
XLA Ops:
  0.0 60.9 %shard_map.73 = f32[128,8,256]{2,1,0:T(8,128)S(1)} custom-call(f32[8,128,256]{2,1,0:T(8,128)} %bg_ref.1, f32[1,256]{1,0:T(1,128)} %bitcast.10, f32[1,256]{1,0:T(1,128)} %bitcast.11, s32[128,512]{1,0:T(8,128)} %bitcast.7, s32[1,128]{1,0:T(1,128)} %count_ref.1, f32[128,512]{1,0:T(8,128)} %bitcast.8, f32[128,512]{1,0:T(8,128)} %bitcast.9), custom_call_target="tpu_custom_call" | custom-call | tf_op jit(solution)/shard_map/pallas_call | solution.py:329
  60.9 1.3 %copy.8 = f32[8,128,256]{2,1,0:T(8,128)} copy(f32[8,128,256]{2,0,1:T(8,128)S(1)} %bitcast.6) | data formatting | bytes 2097152 | tf_op jit(solution)/shard_map/transpose | solution.py:367

commit v5 on v4

--- a/solution.py
+++ b/solution.py
@@ -128,7 +128,7 @@
     strip, side = lax.div(me, 8), lax.rem(lax.div(me, 4), 2)
     lows = [lax.rem(me + index, 4) for index in range(4)]
 
-    def peers(action):
+    def peers(action, same=True, others=True):
         def visit(step, carry):
             action(lax.rem(me + step, groups))
             return carry
@@ -147,11 +147,16 @@
             return carry
 
         if groups != 32:
-            lax.fori_loop(1, groups, visit, 0)
+            if others:
+                lax.fori_loop(1, groups, visit, 0)
         else:
-            lax.fori_loop(0, 4, far, 0)
-            block(4 * side, 1, 0)
-            lax.fori_loop(1, 4, near, 0)
+            if others:
+                lax.fori_loop(1, 4, far, 0)
+            if same:
+                block(4 * (1 - side), 0, 0)
+                block(4 * side, 1, 0)
+            if others:
+                lax.fori_loop(1, 4, near, 0)
 
     def tell(semaphore, peer, **where_to):
         pl.semaphore_signal(semaphore, inc=1, device_id={"mem": peer, **where_to}, device_id_type=MESH)
@@ -261,9 +266,14 @@
         announce()
         exchange_edges()
 
-    peers(lambda peer: pl.when(peer < groups - 2)(lambda: hand_over(last, peer)))
-    peers(lambda peer: pl.when(peer > 1)(lambda: hand_over(0, peer)))
-
+    to_last = lambda peer: pl.when(peer < groups - 2)(lambda: hand_over(last, peer))
+    to_first = lambda peer: pl.when(peer > 1)(lambda: hand_over(0, peer))
+    peers(to_last, same=False)
+    peers(to_first, same=False)
+
+    def send_same():
+        peers(to_last, others=False)
+        peers(to_first, others=False)
 
     for load in loads[local + 2:]:
         load.wait()
@@ -292,6 +302,7 @@
             src_ref=owned.at[chunk, pl.ds(0, bulk)], dst_ref=owned.at[chunk, pl.ds(0, bulk)],
             send_sem=gather_send.at[chunk], recv_sem=gather_recv.at[chunk],
             device_id={"mem": me}, device_id_type=MESH).wait_recv()
+        pl.when(step == 0)(send_same)
         pl.when((step == 0) & (tile == 0))(announce)
 
         def halfway():

time: 62.3 us -> 61.2 us (0.982)
  Pallas kernels: 60.9 us -> 59.8 us
    pallas_call x1, Pallas kernels: 60.9 us -> 59.8 us  [body(): pl.pallas_call(functools.partial(kernel, groups, tiles), out_shape=pltpu....]
where the time goes in v5:
time: 61.2 us; the launch traced here: 61.1 us
  Pallas kernels  59.8 us (98%)
  local copies, waits for them, and re-layouts  1.29 us (2%)
    pallas_call x1, Pallas kernels, body(): pl.pallas_call(functools.partial(kernel, groups, tiles), out_shape=pltpu....  59.8 us
    transpose x1, local copies, waits for them, and re-layouts, body(): return jnp.transpose(result, (1, 0, 2))  1.29 us

profile of v5, /device:TPU:1, one launch (start us, length us, event | category | flops | bytes accessed | tf_op | source)
XLA Modules:
  0.0 61.1 jit_solution(11095557188348930847)
XLA Ops:
  0.0 59.8 %shard_map.73 = f32[128,8,256]{2,1,0:T(8,128)S(1)} custom-call(f32[8,128,256]{2,1,0:T(8,128)} %bg_ref.1, f32[1,256]{1,0:T(1,128)} %bitcast.10, f32[1,256]{1,0:T(1,128)} %bitcast.11, s32[128,512]{1,0:T(8,128)} %bitcast.7, s32[1,128]{1,0:T(1,128)} %count_ref.1, f32[128,512]{1,0:T(8,128)} %bitcast.8, f32[128,512]{1,0:T(8,128)} %bitcast.9), custom_call_target="tpu_custom_call" | custom-call | tf_op jit(solution)/shard_map/pallas_call | solution.py:340
  59.8 1.3 %copy.8 = f32[8,128,256]{2,1,0:T(8,128)} copy(f32[8,128,256]{2,0,1:T(8,128)S(1)} %bitcast.6) | data formatting | bytes 2097152 | tf_op jit(solution)/shard_map/transpose | solution.py:378

commit v6 on v5

--- a/solution.py
+++ b/solution.py
@@ -152,11 +152,10 @@
         else:
             if others:
                 lax.fori_loop(1, 4, far, 0)
+                lax.fori_loop(1, 4, near, 0)
             if same:
                 block(4 * (1 - side), 0, 0)
                 block(4 * side, 1, 0)
-            if others:
-                lax.fori_loop(1, 4, near, 0)
 
     def tell(semaphore, peer, **where_to):
         pl.semaphore_signal(semaphore, inc=1, device_id={"mem": peer, **where_to}, device_id_type=MESH)

time: 61.2 us -> 60.4 us (0.987)
  Pallas kernels: 59.8 us -> 59 us
    pallas_call x1, Pallas kernels: 59.8 us -> 59 us  [body(): pl.pallas_call(functools.partial(kernel, groups, tiles), out_shape=pltpu....]
where the time goes in v6:
time: 60.4 us; the launch traced here: 60.3 us
  Pallas kernels  59 us (98%)
  local copies, waits for them, and re-layouts  1.29 us (2%)
    pallas_call x1, Pallas kernels, body(): pl.pallas_call(functools.partial(kernel, groups, tiles), out_shape=pltpu....  59 us
    transpose x1, local copies, waits for them, and re-layouts, body(): return jnp.transpose(result, (1, 0, 2))  1.29 us

profile of v6, /device:TPU:1, one launch (start us, length us, event | category | flops | bytes accessed | tf_op | source)
XLA Modules:
  0.0 60.3 jit_solution(2309555935609952083)
XLA Ops:
  0.0 59.0 %shard_map.73 = f32[128,8,256]{2,1,0:T(8,128)S(1)} custom-call(f32[8,128,256]{2,1,0:T(8,128)} %bg_ref.1, f32[1,256]{1,0:T(1,128)} %bitcast.10, f32[1,256]{1,0:T(1,128)} %bitcast.11, s32[128,512]{1,0:T(8,128)} %bitcast.7, s32[1,128]{1,0:T(1,128)} %count_ref.1, f32[128,512]{1,0:T(8,128)} %bitcast.8, f32[128,512]{1,0:T(8,128)} %bitcast.9), custom_call_target="tpu_custom_call" | custom-call | tf_op jit(solution)/shard_map/pallas_call | solution.py:339
  59.0 1.3 %copy.8 = f32[8,128,256]{2,1,0:T(8,128)} copy(f32[8,128,256]{2,0,1:T(8,128)S(1)} %bitcast.6) | data formatting | bytes 2097152 | tf_op jit(solution)/shard_map/transpose | solution.py:377
